TPU v7x, 32 devices: a whole 2x2x4 slice. The times are simulated.
32 devices in a mesh: grp: 2 (over x), slc: 16 (over z, y, core).
Axes of the slice: x: 2, y: 2, z: 4, core: 2. Of those that a mesh axis runs over, the one named last changes fastest.
Arguments:
- bitstrings: int32 [1024], P('grp'), parts along dimension 0, may hold values from 0 to 511, as said below
- tree_order: int32 [12], P('grp'), parts along dimension 0, may hold values from 0 to 5, each once
- owners: int32 [12], P('grp'), parts along dimension 0, may hold values from 0 to 15
- slice_assign: int32 [64, 6], P(('grp', 'slc')), parts along dimension 0, may hold values from 0 to 63
- boundary: bfloat16 [1024, 4096], P('grp'), parts along dimension 0, may hold values from -6 to 6
- branch_pool: bfloat16 [32, 64, 4096], P(('grp', 'slc')), parts along dimension 0, may hold values from -0.75 to 0.75
- slice_tensors: bfloat16 [12, 64, 4096], P('grp'), parts along dimension 0, may hold values from -3 to 3
- closing: bfloat16 [8192, 128], P('grp'), parts along dimension 0, may hold values from -0.09375 to 0.09375
Outputs:
- amplitudes: float32 [1024, 128], P(('grp', 'slc')), parts along dimension 0
There are 2 independent parts, one for each index of `grp`. A program takes and returns all parts, laid end to end along the dimension named above; each array names one. Nothing has to cross between parts.
Inputs may be any that keep to these rules, and one draw needn't show every extreme that they name: `bitstrings`: 512 distinct configurations. `tree_order`: a permutation of the sections.
All inputs are finite; a program needn't handle non-finite values.
Results may differ from a plain program's by a relative error of at most 0.0075.
Values may be sent and summed in bfloat16 or wider, within the bound.
A program may use at most 128 MiB of HBM per device.

v0:
```python
import math

import jax
import jax.numpy as jnp
from jax import lax
from jax.sharding import PartitionSpec as P


def spread(block, axis, owner):
    block = jnp.where(lax.axis_index(axis) == owner, block, jnp.zeros_like(block))
    return lax.psum(block, axis)


def local(
    bitstrings, tree_order, owners, slice_assign, boundary, branch_pool, slice_tensors, closing
):
    group_count = lax.axis_size("slc")
    my_index = lax.axis_index("slc")
    slice_count = slice_assign.shape[0]
    bond_dim = branch_pool.shape[1]
    pair_dim = branch_pool.shape[2]
    row_total = bitstrings.shape[0]
    section_count = tree_order.shape[0]
    starts = jnp.take(boundary, bitstrings, axis=0)
    states = jnp.broadcast_to(starts[None], (slice_count, row_total, pair_dim))
    own_branch = branch_pool[0]
    for section_idx in range(section_count):
        branch = spread(own_branch, "slc", owners[section_idx])
        product = jnp.einsum(
            "srab,acb->srcb",
            states.reshape(slice_count, row_total, bond_dim, bond_dim),
            branch.reshape(bond_dim, bond_dim, bond_dim),
            preferred_element_type=jnp.float32,
        )
        table = lax.dynamic_index_in_dim(slice_tensors, tree_order[section_idx], 0, keepdims=False)
        factor = jnp.take(table, slice_assign[:, section_idx], axis=0).astype(jnp.float32)
        states = (product.reshape(slice_count, row_total, pair_dim) * factor[:, None, :]).astype(
            jnp.bfloat16
        )
    inverse = 1.0 / math.sqrt(slice_count * group_count)
    share_rows = row_total // group_count
    partial_amps = jnp.einsum("srw,wo->ro", states, closing, preferred_element_type=jnp.float32)
    totals = lax.psum(partial_amps, "slc")
    summed = lax.dynamic_slice_in_dim(totals, my_index * share_rows, share_rows, 0)
    return summed * inverse


def solution(mesh):
    return jax.shard_map(
        local,
        mesh=mesh,
        in_specs=(
            P("grp"),
            P("grp"),
            P("grp"),
            P(("grp", "slc"), None),
            P("grp", None),
            P(("grp", "slc"), None, None),
            P("grp", None, None),
            P("grp", None),
        ),
        out_specs=P(("grp", "slc"), None),
        check_vma=False,
    )
```

profile of v0, /device:TPU:0, one launch (start us, length us, event | category | flops | bytes accessed | tf_op | source)
XLA Modules:
  0.0 318.9 jit_solution(11319033203107848922)
XLA Ops:
  6.5 1.5 fusion.25
  11.9 2.4 broadcast_select_fusion.6
  14.3 2.1 reshape.99
  16.3 2.9 copy.34
  19.3 2.1 reshape.102
  21.3 2.9 copy.37
  24.2 2.1 reshape.101
  26.3 2.9 copy.36
  29.2 2.1 reshape.100
  31.3 2.9 copy.35
  34.2 1.1 reshape.104
  35.3 2.9 copy.39
  38.2 1.1 reshape.103
  39.4 2.9 copy.38
  42.6 0.7 fusion.24
  55.0 3.2 dynamic-slice_bitcast_fusion.1
  58.2 1.7 gather_fusion.5
  60.2 1.7 gather_fusion.4
  62.2 0.6 gather_fusion.3
  63.9 0.6 gather_fusion.1
  65.7 11.4 %gather_fusion = bf16[512,4096]{1,0:T(8,128)(2,1)} fusion(bf16[512,4096]{1,0:T(8,128)(2,1)} %param.14, s32[1024]{0:T(1024)S(1)} %pad_clamp_fusion.6), kind=kCustom, calls=%fused_computation.6 | custom fusion | bytes 8390656 | tf_op jit(solution)/shard_map/jit(_take)/gather | solution.py:24
  77.1 6.5 %copy.40 = bf16[512,4096]{0,1:T(8,128)(2,1)} copy(bf16[512,4096]{1,0:T(8,128)(2,1)} %gather_fusion) | data formatting | bytes 8388608 | tf_op jit(solution)/shard_map/jit(_take)/gather | solution.py:24
  83.6 2.7 broadcast_select_fusion
  86.3 4.4 %copy.41 = bf16[512,64,64]{0,1,2:T(8,128)(2,1)} copy(bf16[512,64,64]{0,2,1:T(8,128)(2,1)S(1)} %broadcast_select_fusion) | data formatting | bytes 8388608 | tf_op jit(solution)/shard_map/jit(_take)/select_n | solution.py:24
  90.7 95.5 %all-reduce.6.cloned.1.call-done = (bf16[64,64,64]{0,1,2:T(8,128)(2,1)}, bf16[64,64,64]{0,1,2:T(8,128)(2,1)}, bf16[64,64,64]{0,1,2:T(8,128)(2,1)}, bf16[64,64,64...) async-done(((bf16[64,64,64]{0,1,2:T(8,128)(2,1)}, bf16[64,64,64]{0,1,2:T(8,128)(2,1)}, bf16[64,64,64]{0,1,2:T(8,128)(2,1)}, ...) | async-done | bytes 3145744 | tf_op jit(solution)/shard_map/psum | solution.py:11
  186.2 8.7 %fusion.4 = bf16[2,512,64,64]{1,2,0,3:T(8,128)(2,1)} fusion(f32[2,64,64]{1,0,2:T(2,128)S(1)} %copy.43, f32[2,64,64]{1,0,2:T(2,128)S(1)} %copy.42, bf16[512,64,64]{0,1,2:T(8,128)(2,1)} %copy.41, bf16[64,64,64]{0,1,2:T(8,128)(2,1)} %get-tuple-element.12, bf16[64,64,64]{0,1,2:T(8,128)(2,1)} %get-tuple-element.13), kind=kOutput, calls=%fused_computation.16 | convolution fusion | flops 1090519040 | bytes 13697024 | tf_op jit(solution)/shard_map/srab,acb->srcb/dot_general | solution.py:29
  194.9 9.8 %fusion.2 = bf16[2,512,64,64]{1,2,0,3:T(8,128)(2,1)} fusion(f32[2,64,64]{1,0,2:T(2,128)S(1)} %copy.45, bf16[2,512,64,64]{1,2,0,3:T(8,128)(2,1)} %fusion.4, f32[2,64,64]{1,0,2:T(2,128)S(1)} %copy.44, bf16[64,64,64]{0,1,2:T(8,128)(2,1)S(1)} %copy-done.1, bf16[64,64,64]{0,1,2:T(8,128)(2,1)S(1)} %copy-done.2), kind=kOutput, calls=%fused_computation.12 | convolution fusion | flops 1090519040 | bytes 17891328 | tf_op jit(solution)/shard_map/srab,acb->srcb/dot_general | solution.py:29
  204.8 10.4 %convert_reduce_fusion = bf16[512,64,64]{0,1,2:T(8,128)(2,1)} fusion(f32[2,64,64]{1,0,2:T(2,128)S(1)} %copy.47, bf16[2,512,64,64]{1,2,0,3:T(8,128)(2,1)} %fusion.2, f32[2,64,64]{1,0,2:T(2,128)S(1)} %copy.46, bf16[64,64,64]{0,1,2:T(8,128)(2,1)} %get-tuple-element.16, bf16[64,64,64]{0,1,2:T(8,128)(2,1)} %get-tuple-element.17), kind=kOutput, calls=%fused_computation.19 | convolution fusion | flops 1096810496 | bytes 13697024 | tf_op jit(solution)/shard_map/srab,acb->srcb/dot_general | solution.py:29
  215.2 4.5 %copy.48 = bf16[512,64,64]{0,2,1:T(8,128)(2,1)S(1)} copy(bf16[512,64,64]{0,1,2:T(8,128)(2,1)} %convert_reduce_fusion) | data formatting | bytes 8388608 | tf_op jit(solution)/shard_map/srw,wo->ro/reduce_sum | solution.py:42
  219.7 2.0 fusion.26
  221.7 89.0 %all-reduce.4.cloned.1.call-done = f32[512,128]{1,0:T(8,128)} async-done(((f32[512,128]{1,0:T(8,128)}), f32[512,128]{1,0:T(8,128)}) %all-reduce.4.cloned.1.call-update) | async-done | bytes 262160 | tf_op jit(solution)/shard_map/psum | solution.py:43
  310.7 1.3 dynamic-slice_multiply_fusion
  (52 shorter events, 3.5 us)
Async XLA Ops:
  6.5 213.2 %copy-start = (bf16[4096,128]{1,0:T(8,128)(2,1)S(1)}, bf16[4096,128]{1,0:T(8,128)(2,1)}, u32[]{:S(2)}) copy-start(bf16[4096,128]{1,0:T(8,128)(2,1)} %param.17) | copy-start | bytes 3145732
  6.5 179.7 %all-reduce.6.cloned.1.call-start = ((), (), s32[]{:S(2)}) async-start(), calls=%async_computation.1 | async-start | bytes 12582912 | tf_op jit(solution)/shard_map/psum | solution.py:11
  29.2 13.4 %copy-start.4 = (s32[6]{0:T(128)S(1)}, s32[6]{0:T(128)}, u32[]{:S(2)}) copy-start(s32[6]{0:T(128)} %param.11) | copy-start | bytes 76
  29.2 21.6 %copy-start.3 = (s32[2,6]{1,0:T(2,128)S(1)}, s32[2,6]{1,0:T(2,128)}, u32[]{:S(2)}) copy-start(s32[2,6]{1,0:T(2,128)} %param.13) | copy-start | bytes 148
  39.4 26.3 %copy-start.5 = (s32[512]{0:T(512)S(1)}, s32[512]{0:T(512)}, u32[]{:S(2)}) copy-start(s32[512]{0:T(512)} %param.10) | copy-start | bytes 6148
  42.3 268.4 %all-reduce.4.cloned.1.call-start = ((), (), s32[]{:S(2)}) async-start(), calls=%async_computation | async-start | bytes 524288 | tf_op jit(solution)/shard_map/psum | solution.py:43
  186.2 8.7 %copy-start.1 = (bf16[64,64,64]{0,1,2:T(8,128)(2,1)S(1)}, bf16[64,64,64]{0,1,2:T(8,128)(2,1)}, u32[]{:S(2)}) copy-start(bf16[64,64,64]{0,1,2:T(8,128)(2,1)} %get-tuple-element.14) | copy-start | bytes 1572868
  186.2 8.7 %copy-start.2 = (bf16[64,64,64]{0,1,2:T(8,128)(2,1)S(1)}, bf16[64,64,64]{0,1,2:T(8,128)(2,1)}, u32[]{:S(2)}) copy-start(bf16[64,64,64]{0,1,2:T(8,128)(2,1)} %get-tuple-element.15) | copy-start | bytes 1572868
Sparse Core Ops, SparseCore 0:
  42.4 143.7 all-reduce.5
  221.8 88.8 all-reduce.3
where the time goes:
time: 320 us; the launch traced here: 319 us
  waiting for transfers between devices  185 us (58%)
  local copies, waits for them, and re-layouts  67.4 us (21%)
  matrix products  30.9 us (10%)
  between operations  28.8 us (9%)
  other arithmetic  7.01 us (2%)
    psum x1, waiting for transfers between devices, spread(): return lax.psum(block, axis)  95.5 us
    psum x1, waiting for transfers between devices, local(): totals = lax.psum(partial_amps, 'slc')  89 us
    dot_general x3, matrix products, local(): jnp.einsum('srab,acb->srcb', states.reshape(slice_count, row_total, bond_...  28.9 us
    reshape x12, local copies, waits for them, and re-layouts, local(): branch.reshape(bond_dim, bond_dim, bond_dim)  28 us
    gather x2, local copies, waits for them, and re-layouts, local(): starts = jnp.take(boundary, bitstrings, axis=0)  17.9 us
  transfers between devices with their start and end apart: 2, of which 2 were waited for; matrix products, arithmetic and copies ran while one was open for 11% of the time, Pallas kernels for 0%

commit v1 on v0

v1 whole, which is shorter than its diff:
```python
import functools
import math

import jax
import jax.numpy as jnp
from jax import lax
from jax.experimental import pallas as pl
from jax.experimental.pallas import tpu as pltpu
from jax.sharding import PartitionSpec as P

MESH = pl.DeviceIdType.MESH
F32 = jnp.float32
BF16 = jnp.bfloat16
LANES = 128


def dot(left, right, left_dim=1, right_dim=0):
    return lax.dot_general(
        left, right, (((left_dim,), (right_dim,)), ((), ())), preferred_element_type=F32
    )


def split(value):
    high = value.astype(BF16)
    return high, (value - high.astype(F32)).astype(BF16)


def contract(
    n, bond, inverse,
    tree_ref, owner_ref, bits_ref, assign_ref, boundary_hbm, branch_hbm, slices_hbm, closing_hbm,
    out_ref,
    own, perm, held, picks, picks_held, picks_all, rows_in, closing_in, chooser, chosen, starts,
    closing_own, weights, factors, state, total, parts, parts_held,
    load_sem, pick_send, pick_recv, piece_send, piece_recv, part_send, part_recv,
):
    me = lax.axis_index("slc")
    per = LANES // bond
    units = bond // per
    width = held.shape[1]
    lanes = width * LANES
    repeat = n * width // units
    shift = int(math.log2(per))
    low = int(math.log2(bond))
    first_unit = (me // repeat) * width
    row_blocks = boundary_hbm.shape[0]
    sections = tree_ref.shape[0]
    each = picks.shape[0]
    slice_count = picks_all.shape[0]
    out_dim = closing_in.shape[1]

    loads = [
        pltpu.make_async_copy(branch_hbm.at[0], own, load_sem.at[0]),
        pltpu.make_async_copy(boundary_hbm, rows_in.at[pl.ds(0, row_blocks)], load_sem.at[1]),
        pltpu.make_async_copy(
            slices_hbm, rows_in.at[pl.ds(row_blocks, slices_hbm.shape[0])], load_sem.at[2]
        ),
        pltpu.make_async_copy(closing_hbm, closing_in, load_sem.at[3]),
    ]
    for load in loads:
        load.start()

    barrier = pltpu.get_barrier_semaphore()

    def greet(step, carry):
        peer = lax.rem(me + step, n)
        pl.semaphore_signal(barrier, inc=1, device_id={"slc": peer}, device_id_type=MESH)
        return carry

    lax.fori_loop(1, n, greet, 0)

    picks[...] = jnp.zeros_like(picks)
    picks[:, 0:sections] = assign_ref[...]
    picks_held[me] = picks[...]

    loads[0].wait()
    lane16 = lax.broadcasted_iota(jnp.int32, (16, LANES), 1)

    def permute(step, carry):
        rows = pl.ds(pl.multiple_of(step * 16, 16), 16)
        cols = [own[rows, g * LANES : (g + 1) * LANES].astype(F32) for g in range(units)]
        bit = 1
        while bit < units:
            move = bit * per
            upper = (lane16 & move) != 0
            fresh = list(cols)
            for v in range(units):
                if v & bit == 0:
                    w = v + bit
                    fresh[v] = jnp.where(upper, pltpu.roll(cols[w], move, 1), cols[v])
                    fresh[w] = jnp.where(upper, cols[w], pltpu.roll(cols[v], LANES - move, 1))
            cols = fresh
            bit *= 2
        for u in range(units):
            perm[u, rows, :] = cols[u].astype(BF16)
        return carry

    lax.fori_loop(0, bond // 16, permute, 0)

    pl.semaphore_wait(barrier, n - 1)

    def pick_copy(step):
        return pltpu.make_async_remote_copy(
            src_ref=picks, dst_ref=picks_held.at[me],
            send_sem=pick_send.at[step], recv_sem=pick_recv.at[step],
            device_id={"slc": lax.rem(me + step, n)}, device_id_type=MESH,
        )

    def piece_copy(step):
        peer = lax.rem(me + step, n)
        return pltpu.make_async_remote_copy(
            src_ref=perm.at[pl.ds((peer // repeat) * width, width)], dst_ref=held.at[me],
            send_sem=piece_send.at[step], recv_sem=piece_recv.at[step],
            device_id={"slc": peer}, device_id_type=MESH,
        )

    def part_copy(step):
        peer = lax.rem(me + step, n)
        return pltpu.make_async_remote_copy(
            src_ref=parts.at[peer], dst_ref=parts_held.at[me],
            send_sem=part_send.at[step], recv_sem=part_recv.at[step],
            device_id={"slc": peer}, device_id_type=MESH,
        )

    def start_first(step, carry):
        pick_copy(step).start()
        piece_copy(step).start()
        return carry

    lax.fori_loop(1, n, start_first, 0)
    held[me] = perm[pl.ds(first_unit, width)]

    def lane_maps(shape, dim):
        lane = lax.broadcasted_iota(jnp.int32, shape, dim)
        group = (lane & (bond - 1)) >> shift
        half = (lane >> low) & (per - 1)
        local = (lane >> 7) * per + (lane & (per - 1))
        return group, half, local

    block = 2 * LANES
    group, half, local = lane_maps((block, lanes), 1)
    target = group * LANES + half * bond + first_unit * per + local
    target = target - lax.broadcasted_iota(jnp.int32, (block, lanes), 0)

    def build(step, carry):
        chooser[pl.ds(pl.multiple_of(step * block, block), block), :] = jnp.where(
            target == step * block, 1.0, 0.0
        ).astype(BF16)
        return carry

    lax.fori_loop(0, chooser.shape[0] // block, build, 0)
    for load in loads[1:]:
        load.wait()

    tall = rows_in.shape[0] // 2

    def choose(step, carry):
        part = rows_in[pl.ds(step * tall, tall)].reshape(tall * bond, rows_in.shape[2])
        chosen[pl.ds(step * tall, tall)] = dot(part, chooser[...]).astype(BF16).reshape(tall, bond, lanes)
        return carry

    lax.fori_loop(0, 2, choose, 0)
    closing_own[...] = dot(closing_in[...], chooser[...], 0, 0)

    row_total = row_blocks * bond
    order = lax.broadcasted_iota(jnp.int32, (row_total, row_total), 0) == bits_ref[...]
    starts[...] = dot(
        jnp.where(order, 1.0, 0.0).astype(BF16),
        chosen[0:row_blocks].reshape(row_total, lanes), 0, 0,
    ).astype(BF16)

    def end_pick(step, carry):
        pick_copy(step).wait()
        return carry

    lax.fori_loop(1, n, end_pick, 0)
    for idx in range(slice_count // each):
        picks_all[idx * each : (idx + 1) * each, :] = picks_held[idx * repeat + lax.rem(me, repeat)]
    values = lax.broadcasted_iota(jnp.int32, (slice_count, bond), 1)
    for k in range(sections):
        hot = jnp.where(values == picks_all[:, k : k + 1], 1.0, 0.0).astype(BF16)
        factors[k] = dot(hot, chosen[row_blocks + tree_ref[k]])

    for s in range(slice_count):
        state[s * out_dim : (s + 1) * out_dim, :] = (
            closing_own[...] * factors[sections - 1, s : s + 1, :]
        ).astype(BF16)

    group, half, local = lane_maps((bond, lanes), 1)
    expand = jnp.where(
        group * per + half == lax.broadcasted_iota(jnp.int32, (bond, lanes), 0), 1.0, 0.0
    ).astype(BF16)
    same = lane_maps((lanes, lanes), 0)[2] == lane_maps((lanes, lanes), 1)[2]

    def end_piece(step, carry):
        piece_copy(step).wait()
        return carry

    lax.fori_loop(1, n, end_piece, 0)
    for k in range(sections):
        piece = held[owner_ref[k]]
        piece = jnp.concatenate([piece[h] for h in range(width)], axis=1)
        weights[k] = jnp.where(same, dot(piece, expand, 0, 0), 0.0).astype(BF16)

    total[...] = jnp.zeros_like(total)
    some = min(8, slice_count)
    rows_of = some * out_dim

    def section(k, step):
        rows = pl.ds(pl.multiple_of(step * rows_of, rows_of), rows_of)
        product = dot(state[rows, :], weights[k])
        factor = factors[k - 1, pl.ds(pl.multiple_of(step * some, some), some), :]
        for t in range(some):
            piece = product[t * out_dim : (t + 1) * out_dim, :] * factor[t : t + 1, :]
            if k > 1:
                place = pl.ds(pl.multiple_of(step * rows_of + t * out_dim, out_dim), out_dim)
                state[place, :] = piece.astype(BF16)
            else:
                total[...] += piece

    for k in range(sections - 1, 0, -1):

        def one(step, carry, k=k):
            section(k, step)
            return carry

        lax.fori_loop(0, slice_count // some, one, 0)

    high, rest = split(total[...])
    head = dot(high, weights[0]) + dot(rest, weights[0])
    high, rest = split(head)
    amps = dot(starts[...], high, 1, 1) + dot(starts[...], rest, 1, 1)
    parts[...] = amps.reshape(parts.shape).astype(BF16)

    def start_part(step, carry):
        part_copy(step).start()
        return carry

    lax.fori_loop(1, n, start_part, 0)
    parts_held[me] = parts[me]

    def end_part(step, carry):
        part_copy(step).wait()
        return carry

    lax.fori_loop(1, n, end_part, 0)
    summed = parts_held[0].astype(F32)
    for idx in range(1, n):
        summed = summed + parts_held[idx].astype(F32)
    out_ref[...] = summed * inverse


def local(
    n, bitstrings, tree_order, owners, slice_assign, boundary, branch_pool, slice_tensors, closing
):
    each, sections = slice_assign.shape
    bond, pair = branch_pool.shape[1:]
    rows = bitstrings.shape[0]
    out_dim = closing.shape[1]
    per = LANES // bond
    units = bond // per
    width = max(1, units // n)
    repeat = n * width // units
    lanes = width * LANES
    slice_count = each * n // repeat
    share = rows // n
    row_blocks = boundary.shape[0] // bond
    blocks = row_blocks + sections
    vmem = pl.BlockSpec(memory_space=pltpu.VMEM)
    smem = pl.BlockSpec(memory_space=pltpu.SMEM)
    far = pl.BlockSpec(memory_space=pl.ANY)
    return pl.pallas_call(
        functools.partial(contract, n, bond, 1.0 / math.sqrt(each * n)),
        out_shape=jax.ShapeDtypeStruct((share, out_dim), F32),
        in_specs=[smem, smem, vmem, vmem, far, far, far, far],
        out_specs=vmem,
        scratch_shapes=[
            pltpu.VMEM((bond, pair), BF16),
            pltpu.VMEM((units, bond, LANES), BF16),
            pltpu.VMEM((n, width, bond, LANES), BF16),
            pltpu.VMEM((each, LANES), jnp.int32),
            pltpu.VMEM((n, each, LANES), jnp.int32),
            pltpu.VMEM((slice_count, LANES), jnp.int32),
            pltpu.VMEM((blocks, bond, pair), BF16),
            pltpu.VMEM((pair, out_dim), BF16),
            pltpu.VMEM((pair, lanes), BF16),
            pltpu.VMEM((blocks, bond, lanes), BF16),
            pltpu.VMEM((rows, lanes), BF16),
            pltpu.VMEM((out_dim, lanes), F32),
            pltpu.VMEM((sections, lanes, lanes), BF16),
            pltpu.VMEM((sections, slice_count, lanes), F32),
            pltpu.VMEM((slice_count * out_dim, lanes), BF16),
            pltpu.VMEM((out_dim, lanes), F32),
            pltpu.VMEM((n, share, out_dim), BF16),
            pltpu.VMEM((n, share, out_dim), BF16),
            pltpu.SemaphoreType.DMA((4,)),
            pltpu.SemaphoreType.DMA((n,)),
            pltpu.SemaphoreType.DMA((n,)),
            pltpu.SemaphoreType.DMA((n,)),
            pltpu.SemaphoreType.DMA((n,)),
            pltpu.SemaphoreType.DMA((n,)),
            pltpu.SemaphoreType.DMA((n,)),
        ],
        compiler_params=pltpu.CompilerParams(
            collective_id=0, has_side_effects=True, vmem_limit_bytes=56 * 2**20
        ),
        name="contract",
    )(
        tree_order,
        owners,
        bitstrings.reshape(1, rows),
        slice_assign,
        boundary.reshape(row_blocks, bond, pair),
        branch_pool,
        slice_tensors,
        closing,
    )


def solution(mesh):
    return jax.shard_map(
        functools.partial(local, mesh.shape["slc"]),
        mesh=mesh,
        in_specs=(
            P("grp"),
            P("grp"),
            P("grp"),
            P(("grp", "slc"), None),
            P("grp", None),
            P(("grp", "slc"), None, None),
            P("grp", None, None),
            P("grp", None),
        ),
        out_specs=P(("grp", "slc"), None),
        check_vma=False,
    )
```

time: 320 us -> 35.2 us (0.11)
  waiting for transfers between devices: 185 us -> 0 us
  local copies, waits for them, and re-layouts: 67.4 us -> 1.32 us
  Pallas kernels: 0 us -> 33.7 us
  matrix products: 30.9 us -> 0 us
  between operations: 28.8 us -> 0.01 us
  other arithmetic: 7.01 us -> 0 us
    psum x2 -> x0, waiting for transfers between devices: 185 us -> none  [the longest x1 95.5 us: spread(): return lax.psum(block, axis)]
    pallas_call x0 -> x1, Pallas kernels: none -> 33.7 us  [local(): pl.pallas_call(functools.partial(contract, n, bond, 1.0 / math.sqrt(each...]
    dot_general x4 -> x0, matrix products: 30.9 us -> none  [the longest x3 28.9 us: local(): jnp.einsum('srab,acb->srcb', states.reshape(slice_count, row_total, bond_...]
    reshape x12 -> x0, local copies, waits for them, and re-layouts: 28 us -> none  [local(): branch.reshape(bond_dim, bond_dim, bond_dim)]
    gather x8 -> x0, local copies, waits for them, and re-layouts: 23.7 us -> none  [the longest x2 17.9 us: local(): starts = jnp.take(boundary, bitstrings, axis=0)]
    select_n x6 -> x0, other arithmetic: 5.11 us -> none  [the longest x2 2.69 us: local(): starts = jnp.take(boundary, bitstrings, axis=0)]
    reduce_sum x1 -> x0, local copies, waits for them, and re-layouts: 4.53 us -> none  [local(): jnp.einsum('srw,wo->ro', states, closing, preferred_element_type=jnp.floa...]
    select_n x1 -> x0, local copies, waits for them, and re-layouts: 4.37 us -> none  [local(): starts = jnp.take(boundary, bitstrings, axis=0)]
  transfers between devices with their start and end apart: 2 -> 0, of which waited for: 2 -> 0; matrix products, arithmetic and copies ran while one was open for 11% -> 0% of each run, Pallas kernels for 0% -> 0%
where the time goes in v1:
time: 35.2 us; the launch traced here: 35 us
  Pallas kernels  33.7 us (96%)
  local copies, waits for them, and re-layouts  1.32 us (4%)
    pallas_call x1, Pallas kernels, local(): pl.pallas_call(functools.partial(contract, n, bond, 1.0 / math.sqrt(each...  33.7 us
    unnamed x1, local copies, waits for them, and re-layouts  1.32 us

profile of v1, /device:TPU:0, one launch (start us, length us, event | category | flops | bytes accessed | tf_op | source)
XLA Modules:
  0.0 35.0 jit_solution(12416864100520249710)
XLA Ops:
  0.0 33.7 %contract.1 = f32[32,128]{1,0:T(8,128)} custom-call(s32[6]{0:T(128)} %tree_ref.1, s32[6]{0:T(128)} %owner_ref.1, s32[1,512]{1,0:T(1,128)} %bitcast.3, s32[2,6]{1,0:T(2,128)} %assign_ref.1, bf16[8,64,4096]{2,1,0:T(8,128)(2,1)} %bitcast.2, bf16[1,64,4096]{2,1,0:T(8,128)(2,1)} %branch_hbm.1, bf16[6,64,4096]{2,1,0:T(8,128)(2,1)} %slices_hbm.1, ...), custom_call_target="tpu_custom_call" | custom-call | tf_op jit(solution)/shard_map/contract/pallas_call | solution.py:271
  33.7 1.3 %copy.10 = f32[32,128]{1,0:T(8,128)} copy(f32[32,128]{1,0:T(8,128)} %contract.1) | data formatting | bytes 32768

commit v2 on v1

--- a/solution.py
+++ b/solution.py
@@ -30,13 +30,13 @@
     tree_ref, owner_ref, bits_ref, assign_ref, boundary_hbm, branch_hbm, slices_hbm, closing_hbm,
     out_ref,
     own, perm, held, picks, picks_held, picks_all, rows_in, closing_in, chooser, chosen, starts,
-    closing_own, weights, factors, state, total, parts, parts_held,
+    closing_own, weights, factors, state, amps, parts, parts_held,
     load_sem, pick_send, pick_recv, piece_send, piece_recv, part_send, part_recv,
 ):
     me = lax.axis_index("slc")
     per = LANES // bond
     units = bond // per
-    width = held.shape[1]
+    width = len(held)
     lanes = width * LANES
     repeat = n * width // units
     shift = int(math.log2(per))
@@ -105,11 +105,11 @@
             device_id={"slc": lax.rem(me + step, n)}, device_id_type=MESH,
         )
 
-    def piece_copy(step):
-        peer = lax.rem(me + step, n)
+    def piece_copy(step, h):
+        peer = lax.bitwise_xor(me, n - step)
         return pltpu.make_async_remote_copy(
-            src_ref=perm.at[pl.ds((peer // repeat) * width, width)], dst_ref=held.at[me],
-            send_sem=piece_send.at[step], recv_sem=piece_recv.at[step],
+            src_ref=perm.at[(peer // repeat) * width + h], dst_ref=held[h].at[me],
+            send_sem=piece_send.at[h, step], recv_sem=piece_recv.at[h, step],
             device_id={"slc": peer}, device_id_type=MESH,
         )
 
@@ -121,13 +121,19 @@
             device_id={"slc": peer}, device_id_type=MESH,
         )
 
-    def start_first(step, carry):
+    def start_pick(step, carry):
         pick_copy(step).start()
-        piece_copy(step).start()
-        return carry
-
-    lax.fori_loop(1, n, start_first, 0)
-    held[me] = perm[pl.ds(first_unit, width)]
+        return carry
+
+    lax.fori_loop(1, n, start_pick, 0)
+    for h in range(width):
+
+        def start_piece(step, carry, h=h):
+            piece_copy(step, h).start()
+            return carry
+
+        lax.fori_loop(1, n, start_piece, 0)
+        held[h][me] = perm[first_unit + h]
 
     def lane_maps(shape, dim):
         lane = lax.broadcasted_iota(jnp.int32, shape, dim)
@@ -176,60 +182,63 @@
     for idx in range(slice_count // each):
         picks_all[idx * each : (idx + 1) * each, :] = picks_held[idx * repeat + lax.rem(me, repeat)]
     values = lax.broadcasted_iota(jnp.int32, (slice_count, bond), 1)
+    pairs = slice_count // 2
     for k in range(sections):
         hot = jnp.where(values == picks_all[:, k : k + 1], 1.0, 0.0).astype(BF16)
-        factors[k] = dot(hot, chosen[row_blocks + tree_ref[k]])
-
-    for s in range(slice_count):
-        state[s * out_dim : (s + 1) * out_dim, :] = (
-            closing_own[...] * factors[sections - 1, s : s + 1, :]
-        ).astype(BF16)
-
-    group, half, local = lane_maps((bond, lanes), 1)
+        factor = dot(hot, chosen[row_blocks + tree_ref[k]])
+        for h in range(width):
+            for p in range(2):
+                factors[h, k, :, p * LANES : (p + 1) * LANES] = factor[
+                    p * pairs : (p + 1) * pairs, h * LANES : (h + 1) * LANES
+                ]
+
+    for h in range(width):
+        own_closing = closing_own[:, h * LANES : (h + 1) * LANES]
+        own_closing = jnp.concatenate([own_closing, own_closing], axis=1)
+        for s in range(pairs):
+            state[h, s] = (own_closing * factors[h, sections - 1, s : s + 1, :]).astype(BF16)
+
+    group, half, local = lane_maps((bond, LANES), 1)
     expand = jnp.where(
-        group * per + half == lax.broadcasted_iota(jnp.int32, (bond, lanes), 0), 1.0, 0.0
+        group * per + half == lax.broadcasted_iota(jnp.int32, (bond, LANES), 0), 1.0, 0.0
     ).astype(BF16)
-    same = lane_maps((lanes, lanes), 0)[2] == lane_maps((lanes, lanes), 1)[2]
-
-    def end_piece(step, carry):
-        piece_copy(step).wait()
-        return carry
-
-    lax.fori_loop(1, n, end_piece, 0)
-    for k in range(sections):
-        piece = held[owner_ref[k]]
-        piece = jnp.concatenate([piece[h] for h in range(width)], axis=1)
-        weights[k] = jnp.where(same, dot(piece, expand, 0, 0), 0.0).astype(BF16)
-
-    total[...] = jnp.zeros_like(total)
-    some = min(8, slice_count)
-    rows_of = some * out_dim
-
-    def section(k, step):
-        rows = pl.ds(pl.multiple_of(step * rows_of, rows_of), rows_of)
-        product = dot(state[rows, :], weights[k])
-        factor = factors[k - 1, pl.ds(pl.multiple_of(step * some, some), some), :]
-        for t in range(some):
-            piece = product[t * out_dim : (t + 1) * out_dim, :] * factor[t : t + 1, :]
-            if k > 1:
-                place = pl.ds(pl.multiple_of(step * rows_of + t * out_dim, out_dim), out_dim)
-                state[place, :] = piece.astype(BF16)
-            else:
-                total[...] += piece
-
-    for k in range(sections - 1, 0, -1):
-
-        def one(step, carry, k=k):
-            section(k, step)
+    same = lane_maps((LANES, LANES), 0)[2] == lane_maps((LANES, LANES), 1)[2]
+    weights[...] = jnp.zeros_like(weights)
+
+    for h in range(width):
+
+        def end_piece(step, carry, h=h):
+            piece_copy(step, h).wait()
             return carry
 
-        lax.fori_loop(0, slice_count // some, one, 0)
-
-    high, rest = split(total[...])
-    head = dot(high, weights[0]) + dot(rest, weights[0])
-    high, rest = split(head)
-    amps = dot(starts[...], high, 1, 1) + dot(starts[...], rest, 1, 1)
-    parts[...] = amps.reshape(parts.shape).astype(BF16)
+        lax.fori_loop(1, n, end_piece, 0)
+        for k in range(sections - 1, -1, -1):
+            weight = jnp.where(same, dot(held[h][owner_ref[k]], expand, 0, 0), 0.0).astype(BF16)
+            for p in range(2):
+                place = slice(p * LANES, (p + 1) * LANES)
+                weights[k, place, place] = weight
+        for k in range(sections - 1, 0, -1):
+            sums = None
+            for s in range(pairs):
+                piece = dot(state[h, s], weights[k]) * factors[h, k - 1, s : s + 1, :]
+                if k > 1:
+                    state[h, s] = piece.astype(BF16)
+                else:
+                    sums = piece if sums is None else sums + piece
+        sums = sums[:, 0:LANES] + sums[:, LANES:]
+        weight = weights[0, 0:LANES, 0:LANES]
+        high, rest = split(sums)
+        high, rest = split(dot(high, weight) + dot(rest, weight))
+        mine = starts[:, h * LANES : (h + 1) * LANES]
+        amp = dot(
+            jnp.concatenate([mine, mine], axis=1), jnp.concatenate([high, rest], axis=1), 1, 1
+        )
+        if h > 0:
+            amp = amp + amps[...]
+        if h < width - 1:
+            amps[...] = amp
+        else:
+            parts[...] = amp.reshape(parts.shape).astype(BF16)
 
     def start_part(step, carry):
         part_copy(step).start()
@@ -276,7 +285,7 @@
         scratch_shapes=[
             pltpu.VMEM((bond, pair), BF16),
             pltpu.VMEM((units, bond, LANES), BF16),
-            pltpu.VMEM((n, width, bond, LANES), BF16),
+            [pltpu.VMEM((n, bond, LANES), BF16)] * width,
             pltpu.VMEM((each, LANES), jnp.int32),
             pltpu.VMEM((n, each, LANES), jnp.int32),
             pltpu.VMEM((slice_count, LANES), jnp.int32),
@@ -286,17 +295,17 @@
             pltpu.VMEM((blocks, bond, lanes), BF16),
             pltpu.VMEM((rows, lanes), BF16),
             pltpu.VMEM((out_dim, lanes), F32),
-            pltpu.VMEM((sections, lanes, lanes), BF16),
-            pltpu.VMEM((sections, slice_count, lanes), F32),
-            pltpu.VMEM((slice_count * out_dim, lanes), BF16),
-            pltpu.VMEM((out_dim, lanes), F32),
+            pltpu.VMEM((sections, 2 * LANES, 2 * LANES), BF16),
+            pltpu.VMEM((width, sections, slice_count // 2, 2 * LANES), F32),
+            pltpu.VMEM((width, slice_count // 2, out_dim, 2 * LANES), BF16),
+            pltpu.VMEM((rows, out_dim), F32),
             pltpu.VMEM((n, share, out_dim), BF16),
             pltpu.VMEM((n, share, out_dim), BF16),
             pltpu.SemaphoreType.DMA((4,)),
             pltpu.SemaphoreType.DMA((n,)),
             pltpu.SemaphoreType.DMA((n,)),
-            pltpu.SemaphoreType.DMA((n,)),
-            pltpu.SemaphoreType.DMA((n,)),
+            pltpu.SemaphoreType.DMA((width, n)),
+            pltpu.SemaphoreType.DMA((width, n)),
             pltpu.SemaphoreType.DMA((n,)),
             pltpu.SemaphoreType.DMA((n,)),
         ],

time: 35.2 us -> 30.2 us (0.86)
  Pallas kernels: 33.7 us -> 28.6 us
    pallas_call x1, Pallas kernels: 33.7 us -> 28.6 us  [local(): pl.pallas_call(functools.partial(contract, n, bond, 1.0 / math.sqrt(each...]
where the time goes in v2:
time: 30.2 us; the launch traced here: 29.9 us
  Pallas kernels  28.6 us (95%)
  local copies, waits for them, and re-layouts  1.32 us (4%)
    pallas_call x1, Pallas kernels, local(): pl.pallas_call(functools.partial(contract, n, bond, 1.0 / math.sqrt(each...  28.6 us
    unnamed x1, local copies, waits for them, and re-layouts  1.32 us

profile of v2, /device:TPU:0, one launch (start us, length us, event | category | flops | bytes accessed | tf_op | source)
XLA Modules:
  0.0 29.9 jit_solution(5414664715002237956)
XLA Ops:
  0.0 28.6 %contract.1 = f32[32,128]{1,0:T(8,128)} custom-call(s32[6]{0:T(128)} %tree_ref.1, s32[6]{0:T(128)} %owner_ref.1, s32[1,512]{1,0:T(1,128)} %bitcast.3, s32[2,6]{1,0:T(2,128)} %assign_ref.1, bf16[8,64,4096]{2,1,0:T(8,128)(2,1)} %bitcast.2, bf16[1,64,4096]{2,1,0:T(8,128)(2,1)} %branch_hbm.1, bf16[6,64,4096]{2,1,0:T(8,128)(2,1)} %slices_hbm.1, ...), custom_call_target="tpu_custom_call" | custom-call | tf_op jit(solution)/shard_map/contract/pallas_call | solution.py:280
  28.6 1.3 %copy.10 = f32[32,128]{1,0:T(8,128)} copy(f32[32,128]{1,0:T(8,128)} %contract.1) | data formatting | bytes 32768
